TPU v7x, 32 devices: a whole 2x2x4 slice. The times are simulated.
32 devices in a mesh: ra: 4 (over z), dec: 8 (over y, x, core).
Axes of the slice: x: 2, y: 2, z: 4, core: 2. Of those that a mesh axis runs over, the one named last changes fastest.
Arguments:
- forests: bfloat16 [8, 32, 128, 1024], P('ra', 'dec'), may hold values from -6 to 6
- resolution: float32 [8, 32, 128], P('ra', 'dec'), may hold values from 0.3 to 1.2
- pixel_range: int32 [8, 32, 2, 128], P('ra', 'dec'), may hold values from 0 to 1024, as said below
- block_pairs: int32 [4, 8, 40, 3], P('ra', 'dec'), may hold values from -1 to 7, as said below
- block_count: int32 [4, 8], P('ra', 'dec'), may hold values from 10 to 40, as said below
- separation_bin: int32 [4, 8, 40, 128, 128], P('ra', 'dec'), may hold values from 0 to 8
Outputs:
- tile_power: float32 [4, 8, 8, 128], P('ra', 'dec')
- sky_power: float32 [8, 128], replicated
Inputs may be any that keep to these rules, and one draw needn't show every extreme that they name: `pixel_range`: lo < hi for every forest; at least 256 valid pixels. `block_pairs`: each device's list names every one of its own cells once with each of the five offsets (0, 0), (0, 1), (1, -1), (1, 0), (1, 1), in an order drawn from the seed. Slots at or past block_count are ignored. `block_count`: some device has all 40 slots live in every draw.
All inputs are finite; a program needn't handle non-finite values.
Results may differ from a plain program's by a relative error of at most 0.0037.
Values may be sent and summed in bfloat16 or wider, within the bound.
No kernel may reach another device: no remote copies, remote signals or barrier semaphores. Data moves between devices by JAX's collectives and lax.ppermute only.
A program may use at most 64 MiB of HBM per device.

v0:
```python
import jax
import jax.numpy as jnp
from jax import lax
from jax.sharding import PartitionSpec as P

NSEP = 8
NKB = 128


def extended(block, sides, width):
    for axis, dim in sides:
        count = lax.axis_size(axis)
        forward = [(i, i + 1) for i in range(count - 1)]
        backward = [(target, source) for source, target in forward]
        low = lax.ppermute(
            lax.slice_in_dim(block, block.shape[dim] - width, None, axis=dim), axis, forward
        )
        high = lax.ppermute(lax.slice_in_dim(block, 0, width, axis=dim), axis, backward)
        block = jnp.concatenate([low, block, high], axis=dim)
    return block


def from_behind(value, axis, steps):
    count = lax.axis_size(axis)
    leading, last = (max(0, -steps), min(count, count - steps))
    return lax.ppermute(value, axis, [(source, source + steps) for source in range(leading, last)])


def dft_table(length, n_modes):
    sample = jnp.arange(length, dtype=jnp.int32)[:, None]
    mode_index = jnp.arange(n_modes, dtype=jnp.int32)[None, :]
    angles = (sample * mode_index % length).astype(jnp.float32) * (2.0 * jnp.pi / length)
    return jnp.concatenate([jnp.cos(angles), jnp.sin(angles)], axis=1).astype(jnp.bfloat16)


def kbin_table(n_modes, n_bins):
    column = jnp.arange(2 * n_modes, dtype=jnp.int32) % n_modes
    which = column // (n_modes // n_bins)
    return (which[:, None] == jnp.arange(n_bins, dtype=jnp.int32)[None, :]).astype(jnp.float32)


def mask_pixels(flux, pixel_range):
    position = jnp.arange(flux.shape[-1], dtype=jnp.int32)
    lower = pixel_range[..., 0, :][..., None]
    upper = pixel_range[..., 1, :][..., None]
    inside = (position >= lower) & (position < upper)
    return jnp.where(inside, flux, jnp.zeros_like(flux))


def to_spectra(masked, widths, basis):
    length = basis.shape[0]
    n_modes = basis.shape[1] // 2
    raw = jnp.dot(masked, basis, preferred_element_type=jnp.float32)
    wavenum = jnp.arange(n_modes, dtype=jnp.float32) * (2.0 * jnp.pi / length)
    wavenum = jnp.concatenate([wavenum, wavenum])
    window = jnp.exp(-0.5 * (wavenum * widths[..., None]) ** 2)
    return (raw * window).astype(jnp.bfloat16)


def block_term(grid_flat, index_a, index_b, sep_bins):
    n_sep = NSEP
    per_cell = sep_bins.shape[0]
    left = lax.dynamic_index_in_dim(grid_flat, index_a, 0, keepdims=False)
    right = lax.dynamic_index_in_dim(grid_flat, index_b, 0, keepdims=False)
    onehot = (sep_bins[None, :, :] == jnp.arange(n_sep, dtype=jnp.int32)[:, None, None]).astype(
        jnp.bfloat16
    )
    mixed = jnp.dot(
        onehot.reshape(n_sep * per_cell, per_cell), right, preferred_element_type=jnp.float32
    )
    mixed = mixed.reshape(n_sep, per_cell, -1)
    block_sum = jnp.sum(mixed * left.astype(jnp.float32)[None], axis=1)
    pair_counts = jnp.sum(onehot.reshape(n_sep, -1).astype(jnp.float32), axis=1)
    return (block_sum, pair_counts)


def per_device(forests, resolution, pixel_range, block_pairs, block_count, separation_bin):
    cells_ra, cells_dec, per_cell, length = forests.shape
    basis = dft_table(length, length // 2)
    masked = mask_pixels(forests, pixel_range)
    own_spectra = to_spectra(masked, resolution, basis)
    sided = extended(own_spectra, (("dec", 1),), 1)
    above = from_behind(sided[0:1], "ra", -1)
    padded = jnp.concatenate([sided, above], axis=0)
    cols_pad = cells_dec + 2
    grid_flat = padded.reshape(-1, per_cell, length)
    entries = block_pairs[0, 0]
    sep_bins = separation_bin[0, 0]
    live_count = block_count[0, 0]

    def slot_term(slot_index):
        entry_row = entries[slot_index]
        row_a = entry_row[0] // cells_dec
        col_a = entry_row[0] % cells_dec + 1
        index_a = row_a * cols_pad + col_a
        index_b = (row_a + entry_row[1]) * cols_pad + col_a + entry_row[2]
        return block_term(grid_flat, index_a, index_b, sep_bins[slot_index])

    start_value = (jnp.zeros((NSEP, length), jnp.float32), jnp.zeros((NSEP,), jnp.float32))

    def add_live(slot_index, carry):
        block_sum, counts = slot_term(slot_index)
        return (carry[0] + block_sum, carry[1] + counts)

    sums, counts = lax.fori_loop(0, live_count, add_live, start_value)
    binned = jnp.dot(sums, kbin_table(length // 2, NKB), precision=lax.Precision.HIGHEST)
    tile_power = (binned / (per_cell * length)).reshape(1, 1, NSEP, NKB)
    summed, all_counts = lax.psum((binned, counts), ("ra", "dec"))
    sky_power = summed / jnp.maximum(all_counts, 1.0)[:, None]
    return (tile_power, sky_power)


def solution(mesh):
    in_specs = (
        P("ra", "dec", None, None),
        P("ra", "dec", None),
        P("ra", "dec", None, None),
        P("ra", "dec", None, None),
        P("ra", "dec"),
        P("ra", "dec", None, None, None),
    )
    out_specs = (P("ra", "dec", None, None), P())
    return jax.shard_map(
        per_device, mesh=mesh, in_specs=in_specs, out_specs=out_specs, check_vma=False
    )
```

profile of v0, /device:TPU:0, one launch (start us, length us, event | category | flops | bytes accessed | tf_op | source)
XLA Modules:
  0.0 456.6 jit_solution(12260927048021557537)
XLA Ops:
  0.7 8.5 %sine_convert_fusion = (bf16[1024,512]{1,0:T(8,128)(2,1)S(1)}, bf16[1024,512]{1,0:T(8,128)(2,1)S(1)}) fusion(), kind=kLoop, calls=%fused_computation.29 | loop fusion | flops 8388608 | bytes 2097152 | tf_op jit(solution)/shard_map/convert.2
  9.2 2.9 multiply_convert_fusion
  12.2 2.4 collective-permute-start
  14.6 1.3 collective-permute-start.1
  16.1 4.4 collective-permute-done.1
  20.5 1.3 pad_maximum_fusion.1
  21.8 1.3 collective-permute-start.2
  23.2 28.7 %collective-permute-done.2 = bf16[1,6,128,1024]{3,2,1,0:T(8,128)(2,1)} collective-permute-done((bf16[1,6,128,1024]{3,2,1,0:T(8,128)(2,1)}, bf16[1,6,128,1024]{3,2,1,0:T(8,128)(2,1)}, u32[]{:S(2)}, u32[]{:S(2)}) %collective-permute-start.2) | collective-permute-done | bytes 1572896 | tf_op jit(solution)/shard_map/ppermute | solution.py:26
  51.8 3.6 pad_maximum_fusion
  55.4 343.0 %while.14 = (s32[]{:T(128)}, f32[8,1024]{1,0:T(8,128)S(1)}, f32[8]{0:T(128)S(1)}, s32[]{:T(128)}, s32[40,128,128]{2,1,0:T(8,128)}, /*index=5*/s32[40,3]{0,1:T(4,...) while((s32[]{:T(128)}, f32[8,1024]{1,0:T(8,128)S(1)}, ...), condition=%wide.region_3.4_spmd, body=%wide.region_0.3_spmd.sunk | while | flops 271319072 | bytes 2032330 | solution.py:105
  59.3 1.0 bitcast_convert_fusion.2
  62.4 1.7 multiply_reduce_fusion.2
  68.3 1.0 bitcast_convert_fusion.2
  71.5 1.7 multiply_reduce_fusion.2
  77.3 1.0 bitcast_convert_fusion.2
  80.5 1.7 multiply_reduce_fusion.2
  86.3 1.0 bitcast_convert_fusion.2
  89.5 1.7 multiply_reduce_fusion.2
  95.3 1.0 bitcast_convert_fusion.2
  98.5 1.7 multiply_reduce_fusion.2
  104.3 1.0 bitcast_convert_fusion.2
  107.5 1.7 multiply_reduce_fusion.2
  113.3 1.0 bitcast_convert_fusion.2
  116.5 1.7 multiply_reduce_fusion.2
  122.3 1.0 bitcast_convert_fusion.2
  125.5 1.7 multiply_reduce_fusion.2
  131.4 1.0 bitcast_convert_fusion.2
  134.5 1.7 multiply_reduce_fusion.2
  140.4 1.0 bitcast_convert_fusion.2
  143.5 1.7 multiply_reduce_fusion.2
  149.4 1.0 bitcast_convert_fusion.2
  152.5 1.7 multiply_reduce_fusion.2
  158.4 1.0 bitcast_convert_fusion.2
  161.5 1.7 multiply_reduce_fusion.2
  167.4 1.0 bitcast_convert_fusion.2
  170.6 1.7 multiply_reduce_fusion.2
  176.4 1.0 bitcast_convert_fusion.2
  179.6 1.7 multiply_reduce_fusion.2
  185.4 1.0 bitcast_convert_fusion.2
  188.6 1.7 multiply_reduce_fusion.2
  197.6 1.7 multiply_reduce_fusion.2
  206.6 1.7 multiply_reduce_fusion.2
  215.6 1.7 multiply_reduce_fusion.2
  224.6 1.7 multiply_reduce_fusion.2
  233.6 1.7 multiply_reduce_fusion.2
  242.6 1.7 multiply_reduce_fusion.2
  251.6 1.7 multiply_reduce_fusion.2
  260.7 1.7 multiply_reduce_fusion.2
  269.7 1.7 multiply_reduce_fusion.2
  278.7 1.7 multiply_reduce_fusion.2
  287.7 1.7 multiply_reduce_fusion.2
  296.7 1.7 multiply_reduce_fusion.2
  305.7 1.7 multiply_reduce_fusion.2
  314.7 1.7 multiply_reduce_fusion.2
  323.7 1.7 multiply_reduce_fusion.2
  332.7 1.7 multiply_reduce_fusion.2
  341.7 1.7 multiply_reduce_fusion.2
  350.7 1.7 multiply_reduce_fusion.2
  359.8 1.7 multiply_reduce_fusion.2
  368.8 1.7 multiply_reduce_fusion.2
  377.8 1.7 multiply_reduce_fusion.2
  386.8 1.7 multiply_reduce_fusion.2
  395.8 1.7 multiply_reduce_fusion.2
  399.4 56.5 %all-reduce = (f32[8,128]{1,0:T(8,128)S(1)}, f32[8]{0:T(128)S(1)}) all-reduce(f32[8,128]{1,0:T(8,128)S(1)} %fusion.21, f32[8]{0:T(128)S(1)} %get-tuple-element.99), channel_id=1, replica_groups=mesh['ra'=4,'dec'=8] {'ra','dec'}, use_global_device_ids=true, to_apply=%region_4.5 | all-reduce | flops 1032 | bytes 8256 | tf_op jit(solution)/shard_map/psum | solution.py:108
  (272 shorter events, 92.7 us)
Async XLA Ops:
  0.6 8.5 %copy-start = (s32[2,4,2,128]{3,2,1,0:T(2,128)S(1)}, s32[2,4,2,128]{3,2,1,0:T(2,128)}, u32[]{:S(2)}) copy-start(s32[2,4,2,128]{3,2,1,0:T(2,128)} %param.10) | copy-start | bytes 24580
  0.6 8.6 %copy-start.2 = (bf16[2,4,128,1024]{3,2,1,0:T(8,128)(2,1)S(1)}, bf16[2,4,128,1024]{3,2,1,0:T(8,128)(2,1)}, u32[]{:S(2)}) copy-start(bf16[2,4,128,1024]{3,2,1,0:T(8,128)(2,1)} %param.8) | copy-start | bytes 6291460
  0.6 8.6 %copy-start.3 = (f32[2,4,128]{2,1,0:T(4,128)S(1)}, f32[2,4,128]{2,1,0:T(4,128)}, u32[]{:S(2)}) copy-start(f32[2,4,128]{2,1,0:T(4,128)} %param.9) | copy-start | bytes 12292
  12.2 3.9 collective-permute-start
  14.6 8.5 %copy-start.1 = (s32[1,1,40,3]{2,1,3,0:T(1,128)S(1)}, s32[1,1,40,3]{2,1,3,0:T(1,128)}, u32[]{:S(2)}) copy-start(s32[1,1,40,3]{2,1,3,0:T(1,128)} %param.11) | copy-start | bytes 1444
  14.6 5.9 %collective-permute-start.1 = (bf16[2,1,128,1024]{3,2,1,0:T(8,128)(2,1)S(1)}, bf16[2,1,128,1024]{3,2,1,0:T(8,128)(2,1)S(1)}, u32[]{:S(2)}, u32[]{:S(2)}) collective-permute-start(bf16[2,1,128,1024]{3,2,1,0:T(8,128)(2,1)S(1)} %get-tuple-element.122), channel_id=1, source_target_pairs={{1,0},{2,1},{3,2},{4,3},{5,4},{6,5},{7,6},{9,8},{10,9},{11,10},{12... | collective-permute-start | bytes 1572872 | tf_op jit(solution)/shard_map/ppermute | solution.py:18
  21.8 30.0 %collective-permute-start.2 = (bf16[1,6,128,1024]{3,2,1,0:T(8,128)(2,1)}, bf16[1,6,128,1024]{3,2,1,0:T(8,128)(2,1)}, u32[]{:S(2)}, u32[]{:S(2)}) collective-permute-start(bf16[1,6,128,1024]{3,2,1,0:T(8,128)(2,1)} %pad_maximum_fusion.1), channel_id=1, source_target_pairs={{8,0},{16,8},{24,16},{9,1},{17,9},{25,17},{10,2},{18,10},{26,18},{... | collective-permute-start | bytes 4718600 | tf_op jit(solution)/shard_map/ppermute | solution.py:26
where the time goes:
time: 464 us; the launch traced here: 457 us
  loops' own time  174 us (38%)
  matrix products  66.7 us (14%)
  other arithmetic  62.7 us (14%)
  local copies, waits for them, and re-layouts  57.8 us (12%)
  blocking collectives  56.5 us (12%)
  waiting for transfers between devices  33.2 us (7%)
  starting transfers between devices  5 us (1%)
    another operation x1, loops' own time, per_device(): sums, counts = lax.fori_loop(0, live_count, add_live, start_value)  174 us
    dot_general x38, matrix products, block_term(): jnp.dot(onehot.reshape(n_sep * per_cell, per_cell), right, preferred_elem...  63.4 us
    psum x1, blocking collectives, per_device(): summed, all_counts = lax.psum((binned, counts), ('ra', 'dec'))  56.5 us
    mul x38, other arithmetic, block_term(): block_sum = jnp.sum(mixed * left.astype(jnp.float32)[None], axis=1)  37.8 us
    eq x38, local copies, waits for them, and re-layouts, block_term(): sep_bins[None, :, :] == jnp.arange(n_sep, dtype=jnp.int32)[:, None, None]  32.5 us
    ppermute x1, waiting for transfers between devices, from_behind(): lax.ppermute(value, axis, [(source, source + steps) for source in range(l...  28.7 us
    slice x38, local copies, waits for them, and re-layouts, slot_term(): index_b = (row_a + entry_row[1]) * cols_pad + col_a + entry_row[2]  22.3 us
    reduce_sum x38, other arithmetic, block_term(): pair_counts = jnp.sum(onehot.reshape(n_sep, -1).astype(jnp.float32), axis=1)  9.44 us
  transfers between devices with their start and end apart: 3, of which 3 were waited for; matrix products, arithmetic and copies ran while one was open for 0% of the time, Pallas kernels for 0%

commit v1 on v0

--- a/solution.py
+++ b/solution.py
@@ -1,3 +1,4 @@
+import functools
 import jax
 import jax.numpy as jnp
 from jax import lax
@@ -5,6 +6,15 @@
 
 NSEP = 8
 NKB = 128
+
+
+def track_the_notes(work_x, mesh_name, mesh_dim):
+    for p in (mesh_name, mesh_dim):
+        work_x = lax.psum(work_x, axis_name=p)
+    return work_x
+
+
+answer_chains_for = functools.partial(track_the_notes, mesh_name="ra", mesh_dim="dec")
 
 
 def extended(block, sides, width):
@@ -105,7 +115,7 @@
     sums, counts = lax.fori_loop(0, live_count, add_live, start_value)
     binned = jnp.dot(sums, kbin_table(length // 2, NKB), precision=lax.Precision.HIGHEST)
     tile_power = (binned / (per_cell * length)).reshape(1, 1, NSEP, NKB)
-    summed, all_counts = lax.psum((binned, counts), ("ra", "dec"))
+    summed, all_counts = answer_chains_for((binned, counts))
     sky_power = summed / jnp.maximum(all_counts, 1.0)[:, None]
     return (tile_power, sky_power)
 

time: 464 us -> 444 us (0.957)
  blocking collectives: 56.5 us -> 39 us
    psum x1 -> x2, blocking collectives: 56.5 us -> 39 us  [track_the_notes(): work_x = lax.psum(work_x, axis_name=p)]
where the time goes in v1:
time: 444 us; the launch traced here: 437 us
  loops' own time  172 us (39%)
  matrix products  66.6 us (15%)
  other arithmetic  62.7 us (14%)
  local copies, waits for them, and re-layouts  57.1 us (13%)
  blocking collectives  39 us (9%)
  waiting for transfers between devices  33.2 us (7%)
  starting transfers between devices  5 us (1%)
    another operation x1, loops' own time, per_device(): sums, counts = lax.fori_loop(0, live_count, add_live, start_value)  172 us
    dot_general x38, matrix products, block_term(): jnp.dot(onehot.reshape(n_sep * per_cell, per_cell), right, preferred_elem...  63.4 us
    psum x2, blocking collectives, track_the_notes(): work_x = lax.psum(work_x, axis_name=p)  39 us
    mul x38, other arithmetic, block_term(): block_sum = jnp.sum(mixed * left.astype(jnp.float32)[None], axis=1)  37.8 us
    eq x38, local copies, waits for them, and re-layouts, block_term(): sep_bins[None, :, :] == jnp.arange(n_sep, dtype=jnp.int32)[:, None, None]  32.5 us
    ppermute x1, waiting for transfers between devices, from_behind(): lax.ppermute(value, axis, [(source, source + steps) for source in range(l...  28.7 us
    slice x38, local copies, waits for them, and re-layouts, slot_term(): index_b = (row_a + entry_row[1]) * cols_pad + col_a + entry_row[2]  21.6 us
    reduce_sum x38, other arithmetic, block_term(): pair_counts = jnp.sum(onehot.reshape(n_sep, -1).astype(jnp.float32), axis=1)  9.44 us
  transfers between devices with their start and end apart: 3, of which 3 were waited for; matrix products, arithmetic and copies ran while one was open for 0% of the time, Pallas kernels for 0%

profile of v1, /device:TPU:0, one launch (start us, length us, event | category | flops | bytes accessed | tf_op | source)
XLA Modules:
  0.0 436.9 jit_solution(6939876547717823608)
XLA Ops:
  0.7 8.5 %sine_convert_fusion = (bf16[1024,512]{1,0:T(8,128)(2,1)S(1)}, bf16[1024,512]{1,0:T(8,128)(2,1)S(1)}) fusion(), kind=kLoop, calls=%fused_computation.29 | loop fusion | flops 8388608 | bytes 2097152 | tf_op jit(solution)/shard_map/convert.2
  9.2 2.9 multiply_convert_fusion
  12.2 2.4 collective-permute-start
  14.6 1.3 collective-permute-start.1
  16.1 4.4 %collective-permute-done.1 = bf16[2,1,128,1024]{3,2,1,0:T(8,128)(2,1)S(1)} collective-permute-done((bf16[2,1,128,1024]{3,2,1,0:T(8,128)(2,1)S(1)}, bf16[2,1,128,1024]{3,2,1,0:T(8,128)(2,1)S(1)}, u32[]{:S(2)}, u32[]{:S(2)}) %collective-permute-start.1) | collective-permute-done | bytes 524320 | tf_op jit(solution)/shard_map/ppermute | solution.py:28
  20.5 1.4 pad_maximum_fusion.1
  21.9 1.3 collective-permute-start.2
  23.2 28.7 %collective-permute-done.2 = bf16[1,6,128,1024]{3,2,1,0:T(8,128)(2,1)} collective-permute-done((bf16[1,6,128,1024]{3,2,1,0:T(8,128)(2,1)}, bf16[1,6,128,1024]{3,2,1,0:T(8,128)(2,1)}, u32[]{:S(2)}, u32[]{:S(2)}) %collective-permute-start.2) | collective-permute-done | bytes 1572896 | tf_op jit(solution)/shard_map/ppermute | solution.py:36
  51.8 3.6 pad_maximum_fusion
  55.4 340.8 %while.14 = (s32[]{:T(128)}, f32[8,1024]{1,0:T(8,128)S(1)}, f32[8]{0:T(128)S(1)}, s32[]{:T(128)}, s32[40,128,128]{2,1,0:T(8,128)}, /*index=5*/s32[40,3]{0,1:T(4,...) while((s32[]{:T(128)}, f32[8,1024]{1,0:T(8,128)S(1)}, ...), condition=%wide.region_3.4_spmd, body=%wide.region_0.3_spmd.sunk | while | flops 271319072 | bytes 2032330 | solution.py:115
  59.3 1.0 bitcast_convert_fusion.2
  62.4 1.7 multiply_reduce_fusion.2
  68.2 1.0 bitcast_convert_fusion.2
  71.4 1.7 multiply_reduce_fusion.2
  77.2 1.0 bitcast_convert_fusion.2
  80.3 1.7 multiply_reduce_fusion.2
  86.1 1.0 bitcast_convert_fusion.2
  89.3 1.7 multiply_reduce_fusion.2
  95.1 1.0 bitcast_convert_fusion.2
  98.2 1.7 multiply_reduce_fusion.2
  104.0 1.0 bitcast_convert_fusion.2
  107.2 1.7 multiply_reduce_fusion.2
  113.0 1.0 bitcast_convert_fusion.2
  116.1 1.7 multiply_reduce_fusion.2
  121.9 1.0 bitcast_convert_fusion.2
  125.1 1.7 multiply_reduce_fusion.2
  130.9 1.0 bitcast_convert_fusion.2
  134.0 1.7 multiply_reduce_fusion.2
  139.8 1.0 bitcast_convert_fusion.2
  143.0 1.7 multiply_reduce_fusion.2
  148.8 1.0 bitcast_convert_fusion.2
  151.9 1.7 multiply_reduce_fusion.2
  157.7 1.0 bitcast_convert_fusion.2
  160.9 1.7 multiply_reduce_fusion.2
  166.7 1.0 bitcast_convert_fusion.2
  169.8 1.7 multiply_reduce_fusion.2
  175.6 1.0 bitcast_convert_fusion.2
  178.8 1.7 multiply_reduce_fusion.2
  187.7 1.7 multiply_reduce_fusion.2
  196.7 1.7 multiply_reduce_fusion.2
  205.6 1.7 multiply_reduce_fusion.2
  214.6 1.7 multiply_reduce_fusion.2
  223.5 1.7 multiply_reduce_fusion.2
  232.5 1.7 multiply_reduce_fusion.2
  241.4 1.7 multiply_reduce_fusion.2
  250.4 1.7 multiply_reduce_fusion.2
  259.4 1.7 multiply_reduce_fusion.2
  268.3 1.7 multiply_reduce_fusion.2
  277.3 1.7 multiply_reduce_fusion.2
  286.2 1.7 multiply_reduce_fusion.2
  295.2 1.7 multiply_reduce_fusion.2
  304.1 1.7 multiply_reduce_fusion.2
  313.1 1.7 multiply_reduce_fusion.2
  322.0 1.7 multiply_reduce_fusion.2
  331.0 1.7 multiply_reduce_fusion.2
  339.9 1.7 multiply_reduce_fusion.2
  348.9 1.7 multiply_reduce_fusion.2
  357.8 1.7 multiply_reduce_fusion.2
  366.8 1.7 multiply_reduce_fusion.2
  375.7 1.7 multiply_reduce_fusion.2
  384.7 1.7 multiply_reduce_fusion.2
  393.6 1.7 multiply_reduce_fusion.2
  397.2 8.5 %all-reduce.1 = (f32[8,128]{1,0:T(8,128)S(1)}, f32[8]{0:T(128)S(1)}) all-reduce(f32[8,128]{1,0:T(8,128)S(1)} %fusion.21, f32[8]{0:T(128)S(1)} %get-tuple-element.99), channel_id=1, replica_groups=mesh['ra'=4,'dec'=8] {'ra'}, use_global_device_ids=true, to_apply=%region_4.5 | all-reduce | flops 1032 | bytes 8256 | tf_op jit(solution)/shard_map/psum | solution.py:13
  405.7 30.5 %all-reduce = (f32[8,128]{1,0:T(8,128)S(1)}, f32[8]{0:T(128)S(1)}) all-reduce(f32[8,128]{1,0:T(8,128)S(1)} %get-tuple-element.116, f32[8]{0:T(128)S(1)} %get-tuple-element.117), channel_id=1, replica_groups=mesh['ra'=4,'dec'=8] {'dec'}, use_global_device_ids=true, to_apply=%region_5.6 | all-reduce | flops 1032 | bytes 8256 | tf_op jit(solution)/shard_map/psum | solution.py:13
  (273 shorter events, 93.0 us)
Async XLA Ops:
  0.6 8.5 %copy-start = (s32[2,4,2,128]{3,2,1,0:T(2,128)S(1)}, s32[2,4,2,128]{3,2,1,0:T(2,128)}, u32[]{:S(2)}) copy-start(s32[2,4,2,128]{3,2,1,0:T(2,128)} %param.10) | copy-start | bytes 24580
  0.6 8.6 %copy-start.2 = (bf16[2,4,128,1024]{3,2,1,0:T(8,128)(2,1)S(1)}, bf16[2,4,128,1024]{3,2,1,0:T(8,128)(2,1)}, u32[]{:S(2)}) copy-start(bf16[2,4,128,1024]{3,2,1,0:T(8,128)(2,1)} %param.8) | copy-start | bytes 6291460
  0.6 8.6 %copy-start.3 = (f32[2,4,128]{2,1,0:T(4,128)S(1)}, f32[2,4,128]{2,1,0:T(4,128)}, u32[]{:S(2)}) copy-start(f32[2,4,128]{2,1,0:T(4,128)} %param.9) | copy-start | bytes 12292
  12.2 3.9 collective-permute-start
  14.6 8.5 %copy-start.1 = (s32[1,1,40,3]{2,1,3,0:T(1,128)S(1)}, s32[1,1,40,3]{2,1,3,0:T(1,128)}, u32[]{:S(2)}) copy-start(s32[1,1,40,3]{2,1,3,0:T(1,128)} %param.11) | copy-start | bytes 1444
  14.6 5.9 %collective-permute-start.1 = (bf16[2,1,128,1024]{3,2,1,0:T(8,128)(2,1)S(1)}, bf16[2,1,128,1024]{3,2,1,0:T(8,128)(2,1)S(1)}, u32[]{:S(2)}, u32[]{:S(2)}) collective-permute-start(bf16[2,1,128,1024]{3,2,1,0:T(8,128)(2,1)S(1)} %get-tuple-element.124), channel_id=1, source_target_pairs={{1,0},{2,1},{3,2},{4,3},{5,4},{6,5},{7,6},{9,8},{10,9},{11,10},{12... | collective-permute-start | bytes 1572872 | tf_op jit(solution)/shard_map/ppermute | solution.py:28
  21.9 30.0 %collective-permute-start.2 = (bf16[1,6,128,1024]{3,2,1,0:T(8,128)(2,1)}, bf16[1,6,128,1024]{3,2,1,0:T(8,128)(2,1)}, u32[]{:S(2)}, u32[]{:S(2)}) collective-permute-start(bf16[1,6,128,1024]{3,2,1,0:T(8,128)(2,1)} %pad_maximum_fusion.1), channel_id=1, source_target_pairs={{8,0},{16,8},{24,16},{9,1},{17,9},{25,17},{10,2},{18,10},{26,18},{... | collective-permute-start | bytes 4718600 | tf_op jit(solution)/shard_map/ppermute | solution.py:36
